TPU v7x, 256 devices: a whole 4x4x8 slice. The times are simulated.
256 devices in a mesh: chan: 8 (over z), seqo: 4 (over y), seqi: 8 (over x, core).
Axes of the slice: x: 4, y: 4, z: 8, core: 2. Of those that a mesh axis runs over, the one named last changes fastest.
Arguments:
- gate_in: bfloat16 [65536, 4096], P(('seqo', 'seqi'), 'chan'), may hold values from -6 to 6
- value_in: bfloat16 [65536, 4096], P(('seqo', 'seqi'), 'chan'), may hold values from -6 to 6
- out_gate: bfloat16 [65536, 4096], P(('seqo', 'seqi'), 'chan'), may hold values from -6 to 6
- residual: bfloat16 [65536, 4096], P(('seqo', 'seqi'), 'chan'), may hold values from -200 to 200
- filters: bfloat16 [8, 32, 6, 65536], P('chan', ('seqo', 'seqi')), may hold values from -5 to 5
- kept_index: int32 [8, 128], P('chan'), may hold values from -1 to 511, as said below
- kept_owner: int32 [8, 128], P('chan'), may hold values from -1 to 31, as said below
- skip_bias: float32 [4096], P('chan'), may hold values from -1 to 1
- norm_gain: float32 [4096], P('chan'), may hold values from 0.5 to 1.5
Outputs:
- hidden_out: bfloat16 [65536, 4096], P(('seqo', 'seqi'), 'chan')
- normed: bfloat16 [65536, 4096], P(('seqo', 'seqi'), 'chan')
Inputs may be any that keep to these rules, and one draw needn't show every extreme that they name: `kept_index`: row s lists the kept channels of slab s in rising order, distinct, between 64 and 128 of them, followed by -1 in the unused slots; some slab lists exactly 128. `kept_owner`: -1 exactly where kept_index is -1, else a device index along seqo+seqi. Within a slab no device owns more than 6 kept channels, and in every slab some device owns exactly 6.
All inputs are finite; a program needn't handle non-finite values.
Results may differ from a plain program's by a relative error of at most 0.005.
Values may be sent and summed in bfloat16 or wider, within the bound.
A program may use at most 128 MiB of HBM per device.

v0:
```python
import jax
import jax.numpy as jnp
from jax import lax
from jax.sharding import PartitionSpec as P

FA = 512
norm_eps = 1e-06
highest = lax.Precision.HIGHEST


def owner_ranks(owners_row):
    is_live = owners_row >= 0
    slot_count = owners_row.shape[0]
    token_position = jnp.arange(slot_count, dtype=jnp.int32)
    earlier = (
        (owners_row[:, None] == owners_row[None, :])
        & is_live[None, :]
        & (token_position[None, :] < token_position[:, None])
    )
    return jnp.sum(earlier.astype(jnp.int32), axis=1)


def angle_table(first, second, modulus):
    product = first[:, None] * second[None, :] % modulus
    return 2.0 * jnp.pi / modulus * product.astype(jnp.float32)


def causal_convolve(signals, kernels, outer_len):
    channels, length = signals.shape
    inner_len = 2 * length // outer_len
    total_len = outer_len * inner_len
    outer_steps = jnp.arange(outer_len, dtype=jnp.int32)
    half_steps = jnp.arange(outer_len // 2, dtype=jnp.int32)
    inner_steps = jnp.arange(inner_len, dtype=jnp.int32)
    outer_angle = angle_table(outer_steps, half_steps, outer_len)
    twist_angle = angle_table(outer_steps, inner_steps, total_len)
    inner_angle = angle_table(inner_steps, inner_steps, inner_len)
    outer_cos = jnp.cos(outer_angle)
    outer_sin = jnp.sin(outer_angle)
    twist_cos = jnp.cos(twist_angle)
    twist_sin = jnp.sin(twist_angle)
    inner_cos = jnp.cos(inner_angle)
    inner_sin = jnp.sin(inner_angle)
    outer_fwd = jnp.concatenate([outer_cos, -outer_sin], axis=0)
    inner_fwd = jnp.concatenate(
        [
            jnp.concatenate([inner_cos, -inner_sin], axis=1),
            jnp.concatenate([inner_sin, inner_cos], axis=1),
        ],
        axis=0,
    )
    inner_back = jnp.concatenate(
        [
            jnp.concatenate([inner_cos, inner_sin], axis=1),
            jnp.concatenate([-inner_sin, inner_cos], axis=1),
        ],
        axis=0,
    )
    outer_back = jnp.concatenate([outer_cos, -outer_sin], axis=0)

    def forward(series):
        blocks = series.astype(jnp.float32).reshape(channels, outer_len // 2, inner_len)
        first = jnp.einsum("ka,cab->ckb", outer_fwd, blocks, precision=highest)
        first_re = first[:, :outer_len]
        first_im = first[:, outer_len:]
        turned_re = first_re * twist_cos + first_im * twist_sin
        turned_im = first_im * twist_cos - first_re * twist_sin
        stacked = jnp.concatenate([turned_re, turned_im], axis=2)
        spec = jnp.einsum("ckb,bj->ckj", stacked, inner_fwd, precision=highest)
        return (spec[:, :, :inner_len], spec[:, :, inner_len:])

    signal_re, signal_im = forward(signals)
    kernel_re, kernel_im = forward(kernels)
    joint_re = signal_re * kernel_re - signal_im * kernel_im
    joint_im = signal_re * kernel_im + signal_im * kernel_re
    joint = jnp.concatenate([joint_re, joint_im], axis=2)
    back = jnp.einsum("ckj,jb->ckb", joint, inner_back, precision=highest)
    back_re = back[:, :, :inner_len]
    back_im = back[:, :, inner_len:]
    untwist_re = back_re * twist_cos - back_im * twist_sin
    untwist_im = back_im * twist_cos + back_re * twist_sin
    untwisted = jnp.concatenate([untwist_re, untwist_im], axis=1)
    result = jnp.einsum("ka,ckb->cab", outer_back, untwisted, precision=highest)
    return (result / total_len).reshape(channels, length)


def local(
    gate_in, value_in, out_gate, residual, filters, kept_index, kept_owner, skip_bias, norm_gain
):
    tok_rows, slab_width = gate_in.shape
    own_slots = filters.shape[2]
    length = filters.shape[3]
    outer_devices = lax.axis_size("seqo")
    inner_devices = lax.axis_size("seqi")
    owner_count = outer_devices * inner_devices
    gated_prod = (gate_in.astype(jnp.float32) * value_in.astype(jnp.float32)).astype(jnp.bfloat16)
    index_row = kept_index[0]
    owners_row = kept_owner[0]
    is_live = owners_row >= 0
    slot_ranks = owner_ranks(owners_row)
    target = jnp.where(is_live, slot_ranks * owner_count + owners_row, -1)
    buffer_rows = jnp.arange(own_slots * owner_count, dtype=jnp.int32)
    select = (buffer_rows[:, None] == target[None, :]).astype(jnp.bfloat16)
    channel_pos = jnp.arange(slab_width, dtype=jnp.int32)
    spread = ((index_row[:, None] == channel_pos[None, :]) & is_live[:, None]).astype(jnp.bfloat16)
    picker = jnp.dot(select, spread, preferred_element_type=jnp.float32).astype(jnp.bfloat16)
    outgoing = lax.dot_general(
        picker, gated_prod, (((1,), (1,)), ((), ())), preferred_element_type=jnp.float32
    ).astype(jnp.bfloat16)
    incoming = lax.all_to_all(
        outgoing.reshape(own_slots, owner_count, tok_rows),
        ("seqo", "seqi"),
        split_axis=1,
        concat_axis=1,
        tiled=True,
    )
    convolved = causal_convolve(incoming.reshape(own_slots, length), filters[0, 0], FA)
    returned = lax.all_to_all(
        convolved.reshape(own_slots, owner_count, tok_rows),
        ("seqo", "seqi"),
        split_axis=1,
        concat_axis=1,
        tiled=True,
    )
    returned = returned.reshape(own_slots * owner_count, tok_rows)
    safe_target = jnp.where(is_live, target, 0)
    kept_rows = jnp.take(returned, safe_target, axis=0)
    put_at = jnp.where(is_live, index_row, slab_width)
    conv_cols = (
        jnp.zeros((tok_rows, slab_width), jnp.float32).at[:, put_at].set(kept_rows.T, mode="drop")
    )
    gated_wide = gated_prod.astype(jnp.float32)
    mixed_out = out_gate.astype(jnp.float32) * (conv_cols + skip_bias[None, :] * gated_wide)
    hidden_out = (residual.astype(jnp.float32) + mixed_out).astype(jnp.bfloat16)
    hidden_wide = hidden_out.astype(jnp.float32)
    squares = jnp.sum(hidden_wide * hidden_wide, axis=1)
    row_total = lax.psum(squares, "chan")
    width_all = slab_width * lax.axis_size("chan")
    scaling = lax.rsqrt(row_total / width_all + norm_eps)
    normed = (hidden_wide * scaling[:, None] * norm_gain[None, :]).astype(jnp.bfloat16)
    return (hidden_out, normed)


def solution(mesh):
    in_specs = (
        P(("seqo", "seqi"), "chan"),
        P(("seqo", "seqi"), "chan"),
        P(("seqo", "seqi"), "chan"),
        P(("seqo", "seqi"), "chan"),
        P("chan", ("seqo", "seqi"), None, None),
        P("chan", None),
        P("chan", None),
        P("chan"),
        P("chan"),
    )
    out_specs = (P(("seqo", "seqi"), "chan"), P(("seqo", "seqi"), "chan"))
    return jax.shard_map(local, mesh=mesh, in_specs=in_specs, out_specs=out_specs, check_vma=False)
```

profile of v0, /device:TPU:0, one launch (start us, length us, event | category | flops | bytes accessed | tf_op | source)
XLA Modules:
  0.0 187.8 jit_solution(6840904414468012201)
XLA Ops:
  3.5 2.9 %copy.66 = bf16[2048,512]{0,1:T(8,128)(2,1)S(1)} copy(bf16[2048,512]{1,0:T(8,128)(2,1)} %param.9) | data formatting | bytes 4194304 | tf_op args[0]
  6.5 4.6 %copy.67 = bf16[2048,512]{0,1:T(8,128)(2,1)} copy(bf16[2048,512]{1,0:T(8,128)(2,1)} %param.10) | data formatting | bytes 4194304 | tf_op args[1]
  11.1 2.5 %convolution_convert_fusion = bf16[192,2048]{1,0:T(8,128)(2,1)S(1)} fusion(bf16[2048,512]{0,1:T(8,128)(2,1)} %copy.67, bf16[2048,512]{0,1:T(8,128)(2,1)S(1)} %copy.66, s32[128]{0:T(128)S(1)} %bitcast.65, pred[128]{0:T(512)(128)(4,1)S(1)} %get-tuple-element.24, s32[128]{0:T(128)S(1)} %fusion.70), kind=kOutput, calls=%fused_computation.35 | convolution fusion | flops 432660480 | bytes 4981888 | tf_op jit(solution)/shard_map/dot_general | solution.py:107
  15.0 6.2 %all-to-all-start = ((bf16[6,32,2048]{2,0,1:T(8,128)(2,1)}), bf16[6,32,2048]{2,0,1:T(8,128)(2,1)}, u32[]{:S(2)}, u32[]{:S(2)}) async-start(bf16[6,32,2048]{2,0,1:T(8,128)(2,1)} %copy.68), calls=%async_computation | async-start | bytes 2097152 | tf_op jit(solution)/shard_map/all_to_all | solution.py:110
  21.2 1.9 %fusion.54 = f32[512,256]{1,0:T(8,128)S(1)} fusion(), kind=kLoop, calls=%fused_computation.83 | loop fusion | flops 1835008 | bytes 524288 | tf_op jit(solution)/shard_map/cos | solution.py:40
  23.1 1.9 %fusion.53 = f32[512,256]{1,0:T(8,128)S(1)} fusion(), kind=kLoop, calls=%fused_computation.82 | loop fusion | flops 1835008 | bytes 524288 | tf_op jit(solution)/shard_map/sin | solution.py:41
  28.0 1.8 fusion.60
  29.8 2.1 %sine_negate_fusion = (f32[512,256]{1,0:T(8,128)S(1)}, f32[512,256]{1,0:T(8,128)S(1)}) fusion(), kind=kLoop, calls=%fused_computation.64 | loop fusion | flops 1966080 | bytes 1048576 | tf_op jit(solution)/shard_map/neg | solution.py:44
  31.9 4.6 %convolution_bitcast_fusion = f32[6,1024,256]{1,2,0:T(8,128)} fusion(bf16[1,6,256,256]{3,1,2,0:T(8,128)(2,1)S(1)} %bitcast.63, f32[512,256]{1,0:T(8,128)S(1)} %get-tuple-element.26, f32[512,256]{1,0:T(8,128)S(1)} %get-tuple-element.27), kind=kOutput, calls=%fused_computation.33 | convolution fusion | flops 4832100352 | bytes 8126464 | tf_op jit(solution)/shard_map/ka,cab->ckb/dot_general | solution.py:63
  36.5 1.9 all-to-all-done
  38.4 2.7 %copy.69 = bf16[6,32,2048]{2,1,0:T(8,128)(2,1)} copy(bf16[6,32,2048]{2,0,1:T(8,128)(2,1)} %all-to-all-done) | data formatting | bytes 1572864 | tf_op jit(solution)/shard_map/all_to_all | solution.py:110
  41.0 2.8 %reshape.146 = bf16[6,256,256]{2,1,0:T(8,128)(2,1)} reshape(bf16[6,32,2048]{2,1,0:T(8,128)(2,1)} %copy.69) | data formatting | bytes 1572864 | tf_op jit(solution)/shard_map/reshape | solution.py:62
  43.9 4.8 %convolution_bitcast_fusion.1 = f32[6,1024,256]{1,2,0:T(8,128)S(1)} fusion(bf16[6,256,256]{2,1,0:T(8,128)(2,1)} %reshape.146, f32[512,256]{1,0:T(8,128)S(1)} %get-tuple-element.26, f32[512,256]{1,0:T(8,128)S(1)} %get-tuple-element.27), kind=kOutput, calls=%fused_computation.34 | convolution fusion | flops 4832100352 | bytes 8126464 | tf_op jit(solution)/shard_map/ka,cab->ckb/dot_general | solution.py:63
  48.8 2.9 %multiply_add_fusion.3 = (f32[6,512,256]{1,2,0:T(8,128)S(1)}, f32[6,512,256]{1,2,0:T(8,128)S(1)}, f32[6,512,256]{1,2,0:T(8,128)S(1)}, f32[6,512,256]{1,2,0:T(8,128)}) fusion(f32[6,1024,256]{1,2,0:T(8,128)S(1)} %convolution_bitcast_fusion.1, f32[512,256]{0,1:T(8,128)S(1)} %copy-done.8, f32[512,256]{0,1:T(8,128)S(1)} %copy-done.6, f32[6,1024,256]{1,2,0:T(8,128)S(1)} %bitcast.60), kind=kLoop, calls=%fused_computation.32 | loop fusion | flops 9437184 | bytes 26214400 | tf_op jit(solution)/shard_map/add | solution.py:66
  51.7 12.5 %fusion = f32[6,512,512]{1,2,0:T(8,128)S(1)} fusion(f32[6,512,256]{1,2,0:T(8,128)S(1)} %get-tuple-element.17, f32[6,512,256]{1,2,0:T(8,128)S(1)} %get-tuple-element.16, f32[256,256]{0,1:T(8,128)S(1)} %copy-done.12, f32[256,256]{0,1:T(8,128)S(1)} %copy-done.11, f32[256,256]{0,1:T(8,128)S(1)} %fusion.66), kind=kOutput, calls=%fused_computation.2 | convolution fusion | flops 9666035712 | bytes 13369344 | tf_op jit(solution)/shard_map/ckb,bj->ckj/dot_general | solution.py:69
  64.2 12.8 %fusion.4 = f32[6,512,512]{1,2,0:T(8,128)S(1)} fusion(f32[6,512,256]{1,2,0:T(8,128)S(1)} %get-tuple-element.20, f32[6,512,256]{1,2,0:T(8,128)S(1)} %copy-done.3, f32[256,256]{0,1:T(8,128)S(1)} %copy-done.12, f32[256,256]{0,1:T(8,128)S(1)} %copy-done.11, f32[256,256]{0,1:T(8,128)S(1)} %fusion.66), kind=kOutput, calls=%fused_computation.6 | convolution fusion | flops 9666035712 | bytes 13369344 | tf_op jit(solution)/shard_map/ckb,bj->ckj/dot_general | solution.py:69
  77.0 1.6 multiply_subtract_fusion.1
  78.6 14.0 %fusion.8 = f32[6,512,512]{1,2,0:T(8,128)S(1)} fusion(f32[6,512,256]{1,2,0:T(8,128)S(1)} %get-tuple-element.13, f32[6,512,256]{1,2,0:T(8,128)S(1)} %get-tuple-element.12, f32[256,256]{0,1:T(8,128)} %get-tuple-element.29, f32[256,256]{0,1:T(8,128)} %copy-done.10, f32[256,256]{0,1:T(8,128)} %get-tuple-element.28), kind=kOutput, calls=%fused_computation.10 | convolution fusion | flops 9666035712 | bytes 13369344 | tf_op jit(solution)/shard_map/ckj,jb->ckb/dot_general | solution.py:77
  93.7 6.7 %multiply_bitcast_fusion = f32[6,256,256]{1,2,0:T(8,128)} fusion(f32[6,512,256]{1,2,0:T(8,128)S(1)} %get-tuple-element.15, f32[6,512,256]{1,2,0:T(8,128)S(1)} %get-tuple-element.14, f32[512,256]{1,0:T(8,128)S(1)} %get-tuple-element.26, f32[512,256]{1,0:T(8,128)S(1)} %copy-done.5), kind=kOutput, calls=%fused_computation.38 | convolution fusion | flops 4834066432 | bytes 8912896 | tf_op jit(solution)/shard_map/ka,ckb->cab/dot_general | solution.py:83
  100.4 1.9 copy.80
  102.5 2.3 %copy.81 = f32[6,32,2048]{2,0,1:T(8,128)} copy(f32[6,32,2048]{2,1,0:T(8,128)S(1)} %reshape_reshape.3) | data formatting | bytes 3145728 | tf_op jit(solution)/shard_map/reshape;reshape | solution.py:119
  104.8 5.6 %all-to-all-start.1 = ((f32[6,32,2048]{2,0,1:T(8,128)}), f32[6,32,2048]{2,0,1:T(8,128)S(1)}, u32[]{:S(2)}, u32[]{:S(2)}) async-start(f32[6,32,2048]{2,0,1:T(8,128)} %copy.81), calls=%async_computation.1 | async-start | bytes 4194304 | tf_op jit(solution)/shard_map/all_to_all | solution.py:118
  110.4 4.0 %copy.64 = bf16[2048,512]{0,1:T(8,128)(2,1)} copy(bf16[2048,512]{1,0:T(8,128)(2,1)} %param.12) | data formatting | bytes 4194304 | tf_op args[3]
  114.4 4.0 %copy.65 = bf16[2048,512]{0,1:T(8,128)(2,1)} copy(bf16[2048,512]{1,0:T(8,128)(2,1)} %param.11) | data formatting | bytes 4194304 | tf_op args[2]
  118.4 22.1 %all-to-all-done.1 = f32[6,32,2048]{2,0,1:T(8,128)S(1)} async-done(((f32[6,32,2048]{2,0,1:T(8,128)}), f32[6,32,2048]{2,0,1:T(8,128)S(1)}, u32[]{:S(2)}, u32[]{:S(2)}) %all-to-all-start.1) | async-done | bytes 1572896 | tf_op jit(solution)/shard_map/all_to_all | solution.py:118
  140.5 2.1 %copy.82 = f32[6,32,2048]{2,1,0:T(8,128)} copy(f32[6,32,2048]{2,0,1:T(8,128)S(1)} %all-to-all-done.1) | data formatting | bytes 3145728 | tf_op jit(solution)/shard_map/all_to_all | solution.py:118
  142.6 6.2 %scatter_custom_fusion = f32[2048,512]{0,1:T(8,128)} fusion(s32[128]{0:T(128)S(1)} %get-tuple-element.23, f32[]{:T(128)} %constant.60.clone.1, f32[]{:T(128)} %constant.76.clone.1, pred[128]{0:T(512)(128)(4,1)S(1)} %get-tuple-element.25, f32[192,2048]{1,0:T(8,128)} %bitcast.61, s32[1024]{0:T(1024)S(1)} %pad_clamp_fusion), kind=kCustom, calls=%fused_computation.36 | custom fusion | flops 262144 | bytes 5771784 | tf_op jit(solution)/shard_map/scatter | solution.py:130
  148.8 7.6 %fusion.16 = (f32[2048]{0:T(1024)S(1)}, bf16[2048,512]{0,1:T(8,128)(2,1)}) fusion(f32[2048,512]{0,1:T(8,128)} %scatter_custom_fusion, bf16[2048,512]{0,1:T(8,128)(2,1)} %copy.67, bf16[2048,512]{0,1:T(8,128)(2,1)S(1)} %copy-done.1, f32[512]{0:T(512)S(1)} %copy-done.15, bf16[2048,512]{0,1:T(8,128)(2,1)} %copy.65, bf16[2048,512]{0,1:T(8,128)(2,1)} %copy.64), kind=kLoop, calls=%fused_computation.20 | loop fusion | flops 15726592 | bytes 14690304 | tf_op jit(solution)/shard_map/reduce_sum | solution.py:136
  156.4 21.4 %psum.7 = f32[2048]{0:T(1024)S(1)} all-reduce(f32[2048]{0:T(1024)S(1)} %get-tuple-element.10), channel_id=1, replica_groups=mesh['chan'=8,'seqo'=4,'seqi'=8] {'chan'}, use_global_device_ids=true, to_apply=%region_3.4 | all-reduce | flops 2048 | bytes 16384 | tf_op jit(solution)/shard_map/psum | solution.py:137
  177.9 3.9 %copy.83 = bf16[2048,512]{1,0:T(8,128)(2,1)} copy(bf16[2048,512]{0,1:T(8,128)(2,1)} %get-tuple-element.11) | data formatting | bytes 4194304
  181.8 1.8 fusion.18
  183.7 3.9 %copy.84 = bf16[2048,512]{1,0:T(8,128)(2,1)} copy(bf16[2048,512]{0,1:T(8,128)(2,1)} %fusion.18) | data formatting | bytes 4194304
  (54 shorter events, 8.7 us)
Async XLA Ops:
  6.5 7.1 %copy-start = (bf16[2048,512]{0,1:T(8,128)(2,1)}, bf16[2048,512]{0,1:T(8,128)(2,1)S(1)}, u32[]{:S(2)}) copy-start(bf16[2048,512]{0,1:T(8,128)(2,1)S(1)} %copy.66) | copy-start | bytes 6291460
  6.5 4.6 %copy-start.17 = (s32[1,128]{1,0:T(1,128)S(1)}, s32[1,128]{1,0:T(1,128)}, u32[]{:S(2)}) copy-start(s32[1,128]{1,0:T(1,128)} %param.14) | copy-start | bytes 1540
  15.0 16.9 %copy-start.13 = (bf16[1,1,6,65536]{3,2,1,0:T(8,128)(2,1)S(1)}, bf16[1,1,6,65536]{3,2,1,0:T(8,128)(2,1)}, u32[]{:S(2)}) copy-start(bf16[1,1,6,65536]{3,2,1,0:T(8,128)(2,1)} %param.13) | copy-start | bytes 2359300
  15.0 23.4 %all-to-all-start = ((bf16[6,32,2048]{2,0,1:T(8,128)(2,1)}), bf16[6,32,2048]{2,0,1:T(8,128)(2,1)}, u32[]{:S(2)}, u32[]{:S(2)}) async-start(bf16[6,32,2048]{2,0,1:T(8,128)(2,1)} %copy.68), calls=%async_computation | async-start | bytes 2097152 | tf_op jit(solution)/shard_map/all_to_all | solution.py:110
  28.0 36.2 %copy-start.10 = (f32[256,256]{0,1:T(8,128)}, f32[256,256]{0,1:T(8,128)S(1)}, u32[]{:S(2)}) copy-start(f32[256,256]{0,1:T(8,128)S(1)} %fusion.66) | copy-start | bytes 786436
  31.8 12.0 %copy-start.4 = (f32[512,256]{1,0:T(8,128)}, f32[512,256]{1,0:T(8,128)S(1)}, u32[]{:S(2)}) copy-start(f32[512,256]{1,0:T(8,128)S(1)} %get-tuple-element.27) | copy-start | bytes 1572868
  38.3 10.4 %slice-start = ((s8[6291456]{0:T(1024)(128)(4,1)}), s8[2097152]{0:T(1024)(128)(4,1)S(1)}, s32[]{:S(2)}) async-start(s8[6291456]{0:T(1024)(128)(4,1)} %bitcast.59), calls=%async_computation.2 | async-start | bytes 4194304
  43.9 4.9 %slice-start.1 = ((s8[6291456]{0:T(1024)(128)(4,1)}), s8[4194304]{0:T(1024)(128)(4,1)S(1)}, s32[]{:S(2)}) async-start(s8[6291456]{0:T(1024)(128)(4,1)} %bitcast.59), calls=%async_computation.3 | async-start | bytes 8388608
  43.9 4.9 %copy-start.6 = (f32[512,256]{0,1:T(8,128)S(1)}, f32[512,256]{0,1:T(8,128)}, u32[]{:S(2)}) copy-start(f32[512,256]{0,1:T(8,128)} %copy.71) | copy-start | bytes 1572868
  43.9 4.9 %copy-start.8 = (f32[512,256]{0,1:T(8,128)S(1)}, f32[512,256]{0,1:T(8,128)}, u32[]{:S(2)}) copy-start(f32[512,256]{0,1:T(8,128)} %copy.72) | copy-start | bytes 1572868
  48.8 2.9 %copy-start.11 = (f32[256,256]{0,1:T(8,128)S(1)}, f32[256,256]{0,1:T(8,128)}, u32[]{:S(2)}) copy-start(f32[256,256]{0,1:T(8,128)} %get-tuple-element.28) | copy-start | bytes 786436
  48.8 2.9 %copy-start.12 = (f32[256,256]{0,1:T(8,128)S(1)}, f32[256,256]{0,1:T(8,128)}, u32[]{:S(2)}) copy-start(f32[256,256]{0,1:T(8,128)} %get-tuple-element.29) | copy-start | bytes 786436
  51.7 12.5 %copy-start.3 = (f32[6,512,256]{1,2,0:T(8,128)S(1)}, f32[6,512,256]{1,2,0:T(8,128)}, u32[]{:S(2)}) copy-start(f32[6,512,256]{1,2,0:T(8,128)} %get-tuple-element.21) | copy-start | bytes 9437188
  78.6 14.0 %copy-start.7 = (f32[512,256]{0,1:T(8,128)S(1)}, f32[512,256]{0,1:T(8,128)}, u32[]{:S(2)}) copy-start(f32[512,256]{0,1:T(8,128)} %copy.71) | copy-start | bytes 1572868
  78.6 14.0 %copy-start.9 = (f32[512,256]{0,1:T(8,128)S(1)}, f32[512,256]{0,1:T(8,128)}, u32[]{:S(2)}) copy-start(f32[512,256]{0,1:T(8,128)} %copy.72) | copy-start | bytes 1572868
  92.6 1.0 copy-start.5
  104.8 35.7 %all-to-all-start.1 = ((f32[6,32,2048]{2,0,1:T(8,128)}), f32[6,32,2048]{2,0,1:T(8,128)S(1)}, u32[]{:S(2)}, u32[]{:S(2)}) async-start(f32[6,32,2048]{2,0,1:T(8,128)} %copy.81), calls=%async_computation.1 | async-start | bytes 4194304 | tf_op jit(solution)/shard_map/all_to_all | solution.py:118
  114.4 4.0 %copy-start.14 = (s32[1,128]{1,0:T(1,128)S(1)}, s32[1,128]{1,0:T(1,128)}, u32[]{:S(2)}) copy-start(s32[1,128]{1,0:T(1,128)} %param.15) | copy-start | bytes 1540
  142.6 6.2 %copy-start.1 = (bf16[2048,512]{0,1:T(8,128)(2,1)S(1)}, bf16[2048,512]{0,1:T(8,128)(2,1)}, u32[]{:S(2)}) copy-start(bf16[2048,512]{0,1:T(8,128)(2,1)} %copy-done) | copy-start | bytes 6291460
  142.6 6.2 %copy-start.15 = (f32[512]{0:T(512)S(1)}, f32[512]{0:T(512)}, u32[]{:S(2)}) copy-start(f32[512]{0:T(512)} %param.16) | copy-start | bytes 6148
  156.4 25.4 %copy-start.2 = (bf16[2048,512]{0,1:T(8,128)(2,1)S(1)}, bf16[2048,512]{0,1:T(8,128)(2,1)}, u32[]{:S(2)}) copy-start(bf16[2048,512]{0,1:T(8,128)(2,1)} %get-tuple-element.11) | copy-start | bytes 6291460
  156.4 25.4 %copy-start.16 = (f32[512]{0:T(512)S(1)}, f32[512]{0:T(512)}, u32[]{:S(2)}) copy-start(f32[512]{0:T(512)} %param.17) | copy-start | bytes 6148
where the time goes:
time: 191 us; the launch traced here: 188 us
  matrix products  57.9 us (30%)
  local copies, waits for them, and re-layouts  38.8 us (20%)
  other arithmetic  32.7 us (17%)
  waiting for transfers between devices  23.9 us (13%)
  blocking collectives  21.4 us (11%)
  starting transfers between devices  11.8 us (6%)
    dot_general x2, matrix products, forward(): spec = jnp.einsum('ckb,bj->ckj', stacked, inner_fwd, precision=highest)  25.3 us
    unnamed x46, local copies, waits for them, and re-layouts  23.4 us
    all_to_all x1, waiting for transfers between devices, local(): lax.all_to_all(convolved.reshape(own_slots, owner_count, tok_rows), ('seq...  22.1 us
    psum x1, blocking collectives, local(): row_total = lax.psum(squares, 'chan')  21.4 us
    dot_general x1, matrix products, causal_convolve(): back = jnp.einsum('ckj,jb->ckb', joint, inner_back, precision=highest)  14 us
    dot_general x2, matrix products, forward(): first = jnp.einsum('ka,cab->ckb', outer_fwd, blocks, precision=highest)  9.43 us
    reduce_sum x1, other arithmetic, local(): squares = jnp.sum(hidden_wide * hidden_wide, axis=1)  7.64 us
    dot_general x1, matrix products, causal_convolve(): result = jnp.einsum('ka,ckb->cab', outer_back, untwisted, precision=highest)  6.74 us
  transfers between devices with their start and end apart: 2, of which 2 were waited for; matrix products, arithmetic and copies ran while one was open for 12% of the time, Pallas kernels for 0%

commit v1 on v0

--- a/solution.py
+++ b/solution.py
@@ -134,7 +134,7 @@
     hidden_out = (residual.astype(jnp.float32) + mixed_out).astype(jnp.bfloat16)
     hidden_wide = hidden_out.astype(jnp.float32)
     squares = jnp.sum(hidden_wide * hidden_wide, axis=1)
-    row_total = lax.psum(squares, "chan")
+    row_total = jnp.sum(lax.all_gather(squares, "chan"), axis=0)
     width_all = slab_width * lax.axis_size("chan")
     scaling = lax.rsqrt(row_total / width_all + norm_eps)
     normed = (hidden_wide * scaling[:, None] * norm_gain[None, :]).astype(jnp.bfloat16)

time: 191 us -> 200 us (1.047)
  the two profiles are of different devices: /device:TPU:0 before, /device:TPU:32 now
where the time goes in v1:
time: 200 us; the launch traced here: 197 us
  matrix products  57.9 us (29%)
  local copies, waits for them, and re-layouts  38.8 us (19%)
  other arithmetic  34.1 us (17%)
  blocking collectives  27.2 us (14%)
  waiting for transfers between devices  24 us (12%)
  starting transfers between devices  13.5 us (7%)
    all_gather x1, blocking collectives, local(): row_total = jnp.sum(lax.all_gather(squares, 'chan'), axis=0)  27.2 us
    dot_general x2, matrix products, forward(): spec = jnp.einsum('ckb,bj->ckj', stacked, inner_fwd, precision=highest)  25.3 us
    unnamed x46, local copies, waits for them, and re-layouts  23.4 us
    all_to_all x1, waiting for transfers between devices, local(): lax.all_to_all(convolved.reshape(own_slots, owner_count, tok_rows), ('seq...  22.1 us
    dot_general x1, matrix products, causal_convolve(): back = jnp.einsum('ckj,jb->ckb', joint, inner_back, precision=highest)  14 us
    dot_general x2, matrix products, forward(): first = jnp.einsum('ka,cab->ckb', outer_fwd, blocks, precision=highest)  9.42 us
    all_to_all x1, starting transfers between devices, local(): lax.all_to_all(outgoing.reshape(own_slots, owner_count, tok_rows), ('seqo...  7.88 us
    reduce_sum x1, other arithmetic, local(): squares = jnp.sum(hidden_wide * hidden_wide, axis=1)  7.64 us
  transfers between devices with their start and end apart: 2, of which 2 were waited for; matrix products, arithmetic and copies ran while one was open for 12% of the time, Pallas kernels for 0%

profile of v1, /device:TPU:32, one launch (start us, length us, event | category | flops | bytes accessed | tf_op | source)
XLA Modules:
  0.0 196.6 jit_solution(4543693357059099065)
XLA Ops:
  3.5 2.9 %copy.66 = bf16[2048,512]{0,1:T(8,128)(2,1)S(1)} copy(bf16[2048,512]{1,0:T(8,128)(2,1)} %param.9) | data formatting | bytes 4194304 | tf_op args[0]
  6.5 4.6 %copy.67 = bf16[2048,512]{0,1:T(8,128)(2,1)} copy(bf16[2048,512]{1,0:T(8,128)(2,1)} %param.10) | data formatting | bytes 4194304 | tf_op args[1]
  11.1 2.5 %convolution_convert_fusion = bf16[192,2048]{1,0:T(8,128)(2,1)S(1)} fusion(bf16[2048,512]{0,1:T(8,128)(2,1)} %copy.67, bf16[2048,512]{0,1:T(8,128)(2,1)S(1)} %copy.66, s32[128]{0:T(128)S(1)} %bitcast.65, pred[128]{0:T(512)(128)(4,1)S(1)} %get-tuple-element.24, s32[128]{0:T(128)S(1)} %fusion.70), kind=kOutput, calls=%fused_computation.35 | convolution fusion | flops 432660480 | bytes 4981888 | tf_op jit(solution)/shard_map/dot_general | solution.py:107
  15.0 7.9 %all-to-all-start = ((bf16[6,32,2048]{2,0,1:T(8,128)(2,1)}), bf16[6,32,2048]{2,0,1:T(8,128)(2,1)}, u32[]{:S(2)}, u32[]{:S(2)}) async-start(bf16[6,32,2048]{2,0,1:T(8,128)(2,1)} %copy.68), calls=%async_computation | async-start | bytes 2097152 | tf_op jit(solution)/shard_map/all_to_all | solution.py:110
  22.9 1.9 fusion.54
  24.8 1.9 fusion.53
  29.7 1.8 fusion.60
  31.5 2.1 %sine_negate_fusion = (f32[512,256]{1,0:T(8,128)S(1)}, f32[512,256]{1,0:T(8,128)S(1)}) fusion(), kind=kLoop, calls=%fused_computation.64 | loop fusion | flops 1966080 | bytes 1048576 | tf_op jit(solution)/shard_map/neg | solution.py:44
  33.6 4.6 %convolution_bitcast_fusion = f32[6,1024,256]{1,2,0:T(8,128)} fusion(bf16[1,6,256,256]{3,1,2,0:T(8,128)(2,1)S(1)} %bitcast.63, f32[512,256]{1,0:T(8,128)S(1)} %get-tuple-element.26, f32[512,256]{1,0:T(8,128)S(1)} %get-tuple-element.27), kind=kOutput, calls=%fused_computation.33 | convolution fusion | flops 4832100352 | bytes 8126464 | tf_op jit(solution)/shard_map/ka,cab->ckb/dot_general | solution.py:63
  38.2 1.9 all-to-all-done
  40.1 2.7 %copy.69 = bf16[6,32,2048]{2,1,0:T(8,128)(2,1)} copy(bf16[6,32,2048]{2,0,1:T(8,128)(2,1)} %all-to-all-done) | data formatting | bytes 1572864 | tf_op jit(solution)/shard_map/all_to_all | solution.py:110
  42.8 2.8 %reshape.150 = bf16[6,256,256]{2,1,0:T(8,128)(2,1)} reshape(bf16[6,32,2048]{2,1,0:T(8,128)(2,1)} %copy.69) | data formatting | bytes 1572864 | tf_op jit(solution)/shard_map/reshape | solution.py:62
  45.6 4.8 %convolution_bitcast_fusion.1 = f32[6,1024,256]{1,2,0:T(8,128)S(1)} fusion(bf16[6,256,256]{2,1,0:T(8,128)(2,1)} %reshape.150, f32[512,256]{1,0:T(8,128)S(1)} %get-tuple-element.26, f32[512,256]{1,0:T(8,128)S(1)} %get-tuple-element.27), kind=kOutput, calls=%fused_computation.34 | convolution fusion | flops 4832100352 | bytes 8126464 | tf_op jit(solution)/shard_map/ka,cab->ckb/dot_general | solution.py:63
  50.5 2.9 %multiply_add_fusion.3 = (f32[6,512,256]{1,2,0:T(8,128)S(1)}, f32[6,512,256]{1,2,0:T(8,128)S(1)}, f32[6,512,256]{1,2,0:T(8,128)S(1)}, f32[6,512,256]{1,2,0:T(8,128)}) fusion(f32[6,1024,256]{1,2,0:T(8,128)S(1)} %convolution_bitcast_fusion.1, f32[512,256]{0,1:T(8,128)S(1)} %copy-done.8, f32[512,256]{0,1:T(8,128)S(1)} %copy-done.6, f32[6,1024,256]{1,2,0:T(8,128)S(1)} %bitcast.60), kind=kLoop, calls=%fused_computation.32 | loop fusion | flops 9437184 | bytes 26214400 | tf_op jit(solution)/shard_map/add | solution.py:66
  53.4 12.5 %fusion = f32[6,512,512]{1,2,0:T(8,128)S(1)} fusion(f32[6,512,256]{1,2,0:T(8,128)S(1)} %get-tuple-element.17, f32[6,512,256]{1,2,0:T(8,128)S(1)} %get-tuple-element.16, f32[256,256]{0,1:T(8,128)S(1)} %copy-done.12, f32[256,256]{0,1:T(8,128)S(1)} %copy-done.11, f32[256,256]{0,1:T(8,128)S(1)} %fusion.66), kind=kOutput, calls=%fused_computation.2 | convolution fusion | flops 9666035712 | bytes 13369344 | tf_op jit(solution)/shard_map/ckb,bj->ckj/dot_general | solution.py:69
  65.9 12.8 %fusion.4 = f32[6,512,512]{1,2,0:T(8,128)S(1)} fusion(f32[6,512,256]{1,2,0:T(8,128)S(1)} %get-tuple-element.20, f32[6,512,256]{1,2,0:T(8,128)S(1)} %copy-done.3, f32[256,256]{0,1:T(8,128)S(1)} %copy-done.12, f32[256,256]{0,1:T(8,128)S(1)} %copy-done.11, f32[256,256]{0,1:T(8,128)S(1)} %fusion.66), kind=kOutput, calls=%fused_computation.6 | convolution fusion | flops 9666035712 | bytes 13369344 | tf_op jit(solution)/shard_map/ckb,bj->ckj/dot_general | solution.py:69
  78.7 1.6 multiply_subtract_fusion.1
  80.3 14.0 %fusion.8 = f32[6,512,512]{1,2,0:T(8,128)S(1)} fusion(f32[6,512,256]{1,2,0:T(8,128)S(1)} %get-tuple-element.13, f32[6,512,256]{1,2,0:T(8,128)S(1)} %get-tuple-element.12, f32[256,256]{0,1:T(8,128)} %get-tuple-element.29, f32[256,256]{0,1:T(8,128)} %copy-done.10, f32[256,256]{0,1:T(8,128)} %get-tuple-element.28), kind=kOutput, calls=%fused_computation.10 | convolution fusion | flops 9666035712 | bytes 13369344 | tf_op jit(solution)/shard_map/ckj,jb->ckb/dot_general | solution.py:77
  95.4 6.7 %multiply_bitcast_fusion = f32[6,256,256]{1,2,0:T(8,128)} fusion(f32[6,512,256]{1,2,0:T(8,128)S(1)} %get-tuple-element.15, f32[6,512,256]{1,2,0:T(8,128)S(1)} %get-tuple-element.14, f32[512,256]{1,0:T(8,128)S(1)} %get-tuple-element.26, f32[512,256]{1,0:T(8,128)S(1)} %copy-done.5), kind=kOutput, calls=%fused_computation.38 | convolution fusion | flops 4834066432 | bytes 8912896 | tf_op jit(solution)/shard_map/ka,ckb->cab/dot_general | solution.py:83
  102.1 1.9 copy.80
  104.2 2.3 %copy.81 = f32[6,32,2048]{2,0,1:T(8,128)} copy(f32[6,32,2048]{2,1,0:T(8,128)S(1)} %reshape_reshape.3) | data formatting | bytes 3145728 | tf_op jit(solution)/shard_map/reshape;reshape | solution.py:119
  106.5 5.6 %all-to-all-start.1 = ((f32[6,32,2048]{2,0,1:T(8,128)}), f32[6,32,2048]{2,0,1:T(8,128)S(1)}, u32[]{:S(2)}, u32[]{:S(2)}) async-start(f32[6,32,2048]{2,0,1:T(8,128)} %copy.81), calls=%async_computation.1 | async-start | bytes 4194304 | tf_op jit(solution)/shard_map/all_to_all | solution.py:118
  112.1 4.0 %copy.64 = bf16[2048,512]{0,1:T(8,128)(2,1)} copy(bf16[2048,512]{1,0:T(8,128)(2,1)} %param.12) | data formatting | bytes 4194304 | tf_op args[3]
  116.1 4.0 %copy.65 = bf16[2048,512]{0,1:T(8,128)(2,1)} copy(bf16[2048,512]{1,0:T(8,128)(2,1)} %param.11) | data formatting | bytes 4194304 | tf_op args[2]
  120.1 22.1 %all-to-all-done.1 = f32[6,32,2048]{2,0,1:T(8,128)S(1)} async-done(((f32[6,32,2048]{2,0,1:T(8,128)}), f32[6,32,2048]{2,0,1:T(8,128)S(1)}, u32[]{:S(2)}, u32[]{:S(2)}) %all-to-all-start.1) | async-done | bytes 1572896 | tf_op jit(solution)/shard_map/all_to_all | solution.py:118
  142.2 2.1 %copy.82 = f32[6,32,2048]{2,1,0:T(8,128)} copy(f32[6,32,2048]{2,0,1:T(8,128)S(1)} %all-to-all-done.1) | data formatting | bytes 3145728 | tf_op jit(solution)/shard_map/all_to_all | solution.py:118
  144.3 7.5 %scatter_custom_fusion = f32[2048,512]{0,1:T(8,128)} fusion(s32[128]{0:T(128)S(1)} %get-tuple-element.23, f32[]{:T(128)} %constant.60.clone.1, f32[]{:T(128)} %constant.76.clone.1, pred[128]{0:T(512)(128)(4,1)S(1)} %get-tuple-element.25, f32[192,2048]{1,0:T(8,128)} %bitcast.61, s32[1024]{0:T(1024)S(1)} %pad_clamp_fusion), kind=kCustom, calls=%fused_computation.36 | custom fusion | flops 262144 | bytes 5771784 | tf_op jit(solution)/shard_map/scatter | solution.py:130
  151.8 7.6 %fusion.16 = (f32[2048]{0:T(1024)S(1)}, bf16[2048,512]{0,1:T(8,128)(2,1)}) fusion(f32[2048,512]{0,1:T(8,128)} %scatter_custom_fusion, bf16[2048,512]{0,1:T(8,128)(2,1)} %copy.67, bf16[2048,512]{0,1:T(8,128)(2,1)S(1)} %copy-done.1, f32[512]{0:T(512)S(1)} %copy-done.15, bf16[2048,512]{0,1:T(8,128)(2,1)} %copy.65, bf16[2048,512]{0,1:T(8,128)(2,1)} %copy.64), kind=kLoop, calls=%fused_computation.20 | loop fusion | flops 15726592 | bytes 14690304 | tf_op jit(solution)/shard_map/reduce_sum | solution.py:136
  159.5 27.2 %all-gather = f32[16384]{0:T(1024)S(1)} all-gather(f32[2048]{0:T(1024)S(1)} %get-tuple-element.10), channel_id=2, replica_groups=mesh['chan'=8,'seqo'=4,'seqi'=8] {'chan'}, dimensions={0}, use_global_device_ids=true | all-gather | bytes 73728 | tf_op jit(solution)/shard_map/all_gather | solution.py:137
  186.7 3.9 %copy.83 = bf16[2048,512]{1,0:T(8,128)(2,1)} copy(bf16[2048,512]{0,1:T(8,128)(2,1)} %get-tuple-element.11) | data formatting | bytes 4194304
  190.6 1.8 fusion.18
  192.5 3.9 %copy.84 = bf16[2048,512]{1,0:T(8,128)(2,1)} copy(bf16[2048,512]{0,1:T(8,128)(2,1)} %fusion.18) | data formatting | bytes 4194304
  (56 shorter events, 8.7 us)
Async XLA Ops:
  6.5 7.1 %copy-start = (bf16[2048,512]{0,1:T(8,128)(2,1)}, bf16[2048,512]{0,1:T(8,128)(2,1)S(1)}, u32[]{:S(2)}) copy-start(bf16[2048,512]{0,1:T(8,128)(2,1)S(1)} %copy.66) | copy-start | bytes 6291460
  6.5 4.6 %copy-start.17 = (s32[1,128]{1,0:T(1,128)S(1)}, s32[1,128]{1,0:T(1,128)}, u32[]{:S(2)}) copy-start(s32[1,128]{1,0:T(1,128)} %param.14) | copy-start | bytes 1540
  15.0 18.6 %copy-start.13 = (bf16[1,1,6,65536]{3,2,1,0:T(8,128)(2,1)S(1)}, bf16[1,1,6,65536]{3,2,1,0:T(8,128)(2,1)}, u32[]{:S(2)}) copy-start(bf16[1,1,6,65536]{3,2,1,0:T(8,128)(2,1)} %param.13) | copy-start | bytes 2359300
  15.0 25.1 %all-to-all-start = ((bf16[6,32,2048]{2,0,1:T(8,128)(2,1)}), bf16[6,32,2048]{2,0,1:T(8,128)(2,1)}, u32[]{:S(2)}, u32[]{:S(2)}) async-start(bf16[6,32,2048]{2,0,1:T(8,128)(2,1)} %copy.68), calls=%async_computation | async-start | bytes 2097152 | tf_op jit(solution)/shard_map/all_to_all | solution.py:110
  29.7 36.2 %copy-start.10 = (f32[256,256]{0,1:T(8,128)}, f32[256,256]{0,1:T(8,128)S(1)}, u32[]{:S(2)}) copy-start(f32[256,256]{0,1:T(8,128)S(1)} %fusion.66) | copy-start | bytes 786436
  33.6 12.0 %copy-start.4 = (f32[512,256]{1,0:T(8,128)}, f32[512,256]{1,0:T(8,128)S(1)}, u32[]{:S(2)}) copy-start(f32[512,256]{1,0:T(8,128)S(1)} %get-tuple-element.27) | copy-start | bytes 1572868
  40.1 10.4 %slice-start = ((s8[6291456]{0:T(1024)(128)(4,1)}), s8[2097152]{0:T(1024)(128)(4,1)S(1)}, s32[]{:S(2)}) async-start(s8[6291456]{0:T(1024)(128)(4,1)} %bitcast.59), calls=%async_computation.2 | async-start | bytes 4194304
  45.6 4.9 %slice-start.1 = ((s8[6291456]{0:T(1024)(128)(4,1)}), s8[4194304]{0:T(1024)(128)(4,1)S(1)}, s32[]{:S(2)}) async-start(s8[6291456]{0:T(1024)(128)(4,1)} %bitcast.59), calls=%async_computation.3 | async-start | bytes 8388608
  45.6 4.9 %copy-start.6 = (f32[512,256]{0,1:T(8,128)S(1)}, f32[512,256]{0,1:T(8,128)}, u32[]{:S(2)}) copy-start(f32[512,256]{0,1:T(8,128)} %copy.71) | copy-start | bytes 1572868
  45.6 4.9 %copy-start.8 = (f32[512,256]{0,1:T(8,128)S(1)}, f32[512,256]{0,1:T(8,128)}, u32[]{:S(2)}) copy-start(f32[512,256]{0,1:T(8,128)} %copy.72) | copy-start | bytes 1572868
  50.5 2.9 %copy-start.11 = (f32[256,256]{0,1:T(8,128)S(1)}, f32[256,256]{0,1:T(8,128)}, u32[]{:S(2)}) copy-start(f32[256,256]{0,1:T(8,128)} %get-tuple-element.28) | copy-start | bytes 786436
  50.5 2.9 %copy-start.12 = (f32[256,256]{0,1:T(8,128)S(1)}, f32[256,256]{0,1:T(8,128)}, u32[]{:S(2)}) copy-start(f32[256,256]{0,1:T(8,128)} %get-tuple-element.29) | copy-start | bytes 786436
  53.4 12.5 %copy-start.3 = (f32[6,512,256]{1,2,0:T(8,128)S(1)}, f32[6,512,256]{1,2,0:T(8,128)}, u32[]{:S(2)}) copy-start(f32[6,512,256]{1,2,0:T(8,128)} %get-tuple-element.21) | copy-start | bytes 9437188
  80.3 14.0 %copy-start.7 = (f32[512,256]{0,1:T(8,128)S(1)}, f32[512,256]{0,1:T(8,128)}, u32[]{:S(2)}) copy-start(f32[512,256]{0,1:T(8,128)} %copy.71) | copy-start | bytes 1572868
  80.3 14.0 %copy-start.9 = (f32[512,256]{0,1:T(8,128)S(1)}, f32[512,256]{0,1:T(8,128)}, u32[]{:S(2)}) copy-start(f32[512,256]{0,1:T(8,128)} %copy.72) | copy-start | bytes 1572868
  94.3 1.0 copy-start.5
  106.5 35.7 %all-to-all-start.1 = ((f32[6,32,2048]{2,0,1:T(8,128)}), f32[6,32,2048]{2,0,1:T(8,128)S(1)}, u32[]{:S(2)}, u32[]{:S(2)}) async-start(f32[6,32,2048]{2,0,1:T(8,128)} %copy.81), calls=%async_computation.1 | async-start | bytes 4194304 | tf_op jit(solution)/shard_map/all_to_all | solution.py:118
  116.1 4.0 %copy-start.14 = (s32[1,128]{1,0:T(1,128)S(1)}, s32[1,128]{1,0:T(1,128)}, u32[]{:S(2)}) copy-start(s32[1,128]{1,0:T(1,128)} %param.15) | copy-start | bytes 1540
  144.3 7.5 %copy-start.1 = (bf16[2048,512]{0,1:T(8,128)(2,1)S(1)}, bf16[2048,512]{0,1:T(8,128)(2,1)}, u32[]{:S(2)}) copy-start(bf16[2048,512]{0,1:T(8,128)(2,1)} %copy-done) | copy-start | bytes 6291460
  144.3 7.6 %copy-start.15 = (f32[512]{0:T(512)S(1)}, f32[512]{0:T(512)}, u32[]{:S(2)}) copy-start(f32[512]{0:T(512)} %param.16) | copy-start | bytes 6148
  159.5 31.2 %copy-start.2 = (bf16[2048,512]{0,1:T(8,128)(2,1)S(1)}, bf16[2048,512]{0,1:T(8,128)(2,1)}, u32[]{:S(2)}) copy-start(bf16[2048,512]{0,1:T(8,128)(2,1)} %get-tuple-element.11) | copy-start | bytes 6291460
  159.5 31.2 %copy-start.16 = (f32[512]{0:T(512)S(1)}, f32[512]{0:T(512)}, u32[]{:S(2)}) copy-start(f32[512]{0:T(512)} %param.17) | copy-start | bytes 6148
